TPU v7x, 128 devices: a whole 4x4x4 slice. The times are simulated.
128 devices in a mesh: tile: 64 (over z, x, y_lo, core), chan: 2 (over y_hi).
Axes of the slice: x: 4, y: 4 (y_hi: 2, y_lo: 2; y = y_hi * 2 + y_lo), z: 4, core: 2. Of those that a mesh axis runs over, the one named last changes fastest.
Arguments:
- inputs: bfloat16 [128, 64, 4096], P('tile', 'chan'), may hold values from -6 to 6
- gluing: int32 [128, 4, 3], P('tile'), may hold values from 0 to 127, as said below
- conv_weight: bfloat16 [64, 64, 3, 3], replicated, may hold values from -0.25 to 0.25
- level_weight: bfloat16 [128, 64, 2, 2], replicated, may hold values from -0.375 to 0.375
- cotangent: bfloat16 [128, 128, 1024], P('tile', 'chan'), may hold values from -6 to 6
Outputs:
- level: bfloat16 [128, 128, 1024], P('tile', 'chan')
- grad_inputs: bfloat16 [128, 64, 4096], P('tile', 'chan')
- grad_conv: float32 [64, 64, 3, 3], P(None, 'chan')
- grad_level: float32 [128, 64, 2, 2], P(None, 'chan')
Inputs may be any that keep to these rules, and one draw needn't show every extreme that they name: Entry [t, s] = (u, r, f) with r in 0..3 and f in 0..1 says that side s of tile t is glued to side r of tile u; the gluing is symmetric: entry [u, r] is (t, s, f), and no side is glued to itself.
All inputs are finite; a program needn't handle non-finite values.
Results may differ from a plain program's by a relative error of at most 0.005.
Values may be sent and summed in bfloat16 or wider, within the bound.
No kernel may reach another device: no remote copies, remote signals or barrier semaphores. Data moves between devices by JAX's collectives and lax.ppermute only.
A program may use at most 128 MiB of HBM per device.

v0:
```python
import jax
import jax.numpy as jnp
from jax import lax
from jax.sharding import PartitionSpec as P

S = 64


def edge_strips(source):
    return jnp.stack(
        [source[:, :, 0, :], source[:, :, -1, :], source[:, :, :, 0], source[:, :, :, -1]], axis=1
    )


def border_strips(padded):
    return jnp.stack(
        [
            padded[:, :, 0, 1:-1],
            padded[:, :, -1, 1:-1],
            padded[:, :, 1:-1, 0],
            padded[:, :, 1:-1, -1],
        ],
        axis=1,
    )


def orient(strips, gluing):
    return jnp.where(gluing[:, :, 2][:, :, None, None] == 1, strips[..., ::-1], strips)


def make_picker(gluing):
    target = gluing[:, :, 0] * 4 + gluing[:, :, 1]

    def picker(current, received, first_row):
        strip_count = received.shape[0] * 4
        received_rows = received.reshape((strip_count,) + received.shape[2:])
        inside = (target >= 0) & (target < strip_count)
        chosen = jnp.take(received_rows, jnp.clip(target, 0, strip_count - 1), axis=0)
        return jnp.where(inside[:, :, None, None], chosen, current)

    return picker


def assemble(source, halo_cells):
    tile_count, chan_count = (source.shape[0], source.shape[1])
    corner = jnp.zeros((tile_count, chan_count, 1), source.dtype)
    top_row = jnp.concatenate([corner, halo_cells[:, 0], corner], axis=2)[:, :, None, :]
    low_row = jnp.concatenate([corner, halo_cells[:, 1], corner], axis=2)[:, :, None, :]
    middle = jnp.concatenate(
        [halo_cells[:, 2][:, :, :, None], source, halo_cells[:, 3][:, :, :, None]], axis=3
    )
    return jnp.concatenate([top_row, middle, low_row], axis=2)


def conv_three(padded, weight):
    extent = padded.shape[2] - 2
    summed = None
    for row_tap in range(3):
        for col_tap in range(3):
            product_term = jnp.einsum(
                "oc,ncxy->noxy",
                weight[:, :, row_tap, col_tap],
                padded[:, :, row_tap : row_tap + extent, col_tap : col_tap + extent],
                preferred_element_type=jnp.float32,
            )
            summed = product_term if summed is None else summed + product_term
    return summed


def conv_two(hidden, weight):
    tile_count, chan_count, extent = (hidden.shape[0], hidden.shape[1], hidden.shape[2])
    summed = None
    for row_tap in range(2):
        for col_tap in range(2):
            sampled = hidden[:, :, row_tap::2, col_tap::2].reshape(tile_count, chan_count, -1)
            product_term = jnp.einsum(
                "oc,ncp->nop",
                weight[:, :, row_tap, col_tap],
                sampled,
                preferred_element_type=jnp.float32,
            )
            summed = product_term if summed is None else summed + product_term
    return summed.reshape(tile_count, weight.shape[0], extent // 2, extent // 2)


def level_grads(hidden, cot_full, weight):
    tile_count, chan_count, extent = (hidden.shape[0], hidden.shape[1], hidden.shape[2])
    half = extent // 2
    cot_rows = cot_full.reshape(tile_count, cot_full.shape[1], -1)
    weight_rows = []
    spread_rows = []
    for row_tap in range(2):
        weight_cols = []
        spread_cols = []
        for col_tap in range(2):
            sampled = hidden[:, :, row_tap::2, col_tap::2].reshape(tile_count, chan_count, -1)
            weight_cols.append(
                jnp.einsum("nop,ncp->oc", cot_rows, sampled, preferred_element_type=jnp.float32)
            )
            spread = jnp.einsum(
                "oc,nop->ncp",
                weight[:, :, row_tap, col_tap],
                cot_rows,
                preferred_element_type=jnp.float32,
            )
            spread_cols.append(spread.reshape(tile_count, chan_count, half, half))
        weight_rows.append(jnp.stack(weight_cols, axis=-1))
        spread_rows.append(jnp.stack(spread_cols, axis=-1))
    grad_weight = jnp.stack(weight_rows, axis=2)
    grad_hidden = jnp.stack(spread_rows, axis=3).reshape(tile_count, chan_count, extent, extent)
    return (grad_weight, grad_hidden)


def conv_grads(padded, grad_full, weight):
    extent = padded.shape[2] - 2
    grad_padded = jnp.zeros(padded.shape, jnp.float32)
    weight_rows = []
    for row_tap in range(3):
        weight_cols = []
        for col_tap in range(3):
            window = padded[:, :, row_tap : row_tap + extent, col_tap : col_tap + extent]
            weight_cols.append(
                jnp.einsum("noxy,ncxy->oc", grad_full, window, preferred_element_type=jnp.float32)
            )
            spread = jnp.einsum(
                "oc,noxy->ncxy",
                weight[:, :, row_tap, col_tap],
                grad_full,
                preferred_element_type=jnp.float32,
            )
            grad_padded = grad_padded.at[
                :, :, row_tap : row_tap + extent, col_tap : col_tap + extent
            ].add(spread)
        weight_rows.append(jnp.stack(weight_cols, axis=-1))
    return (jnp.stack(weight_rows, axis=2), grad_padded)


def add_returned(grad_padded, returned):
    interior = grad_padded[:, :, 1:-1, 1:-1]
    interior = interior.at[:, :, 0, :].add(returned[:, 0])
    interior = interior.at[:, :, -1, :].add(returned[:, 1])
    interior = interior.at[:, :, :, 0].add(returned[:, 2])
    interior = interior.at[:, :, :, -1].add(returned[:, 3])
    return interior.astype(jnp.bfloat16)


def flatten_pixels(field):
    return field.reshape(field.shape[0], field.shape[1], -1)


def on_device(inputs, gluing, conv_weight, level_weight, cotangent):
    inputs = inputs.reshape(inputs.shape[0], inputs.shape[1], S, S)
    cotangent = cotangent.reshape(cotangent.shape[0], cotangent.shape[1], S // 2, S // 2)
    chan_width = inputs.shape[1]
    chan_first = lax.axis_index("chan") * chan_width
    picker = make_picker(gluing)
    conv_in = lax.dynamic_slice_in_dim(conv_weight, chan_first, chan_width, 1)
    level_in = lax.dynamic_slice_in_dim(level_weight, chan_first, chan_width, 1)
    strips = edge_strips(inputs)
    halo_cells = picker(
        jnp.zeros_like(strips), lax.all_gather(strips, "tile", axis=0, tiled=True), jnp.int32(0)
    )
    padded_own = assemble(inputs, orient(halo_cells, gluing))
    partial_pre = conv_three(padded_own, conv_in)
    pre_act = lax.psum_scatter(partial_pre, "chan", scatter_dimension=1, tiled=True)
    hidden = jax.nn.gelu(pre_act).astype(jnp.bfloat16)
    level_part = conv_two(hidden, level_in)
    level = lax.psum_scatter(level_part, "chan", scatter_dimension=1, tiled=True).astype(
        jnp.bfloat16
    )
    cot_full = lax.all_gather(cotangent, "chan", axis=1, tiled=True)
    grad_level, grad_hidden = level_grads(hidden, cot_full, level_in)
    unused, pullback = jax.vjp(jax.nn.gelu, pre_act)
    grad_pre = pullback(grad_hidden)[0].astype(jnp.bfloat16)
    grad_full = lax.all_gather(grad_pre, "chan", axis=1, tiled=True)
    grad_conv, grad_padded = conv_grads(padded_own, grad_full, conv_in)
    grad_conv, grad_level = lax.psum((grad_conv, grad_level), "tile")
    rims = border_strips(grad_padded).astype(jnp.bfloat16)
    returned = picker(
        jnp.zeros_like(rims), lax.all_gather(rims, "tile", axis=0, tiled=True), jnp.int32(0)
    )
    returned = orient(returned, gluing).astype(jnp.float32)
    grad_inputs = add_returned(grad_padded, returned)
    return (flatten_pixels(level), flatten_pixels(grad_inputs), grad_conv, grad_level)


def solution(mesh):
    return jax.shard_map(
        on_device,
        mesh=mesh,
        in_specs=(
            P("tile", "chan", None),
            P("tile", None, None),
            P(),
            P(),
            P("tile", "chan", None),
        ),
        out_specs=(
            P("tile", "chan", None),
            P("tile", "chan", None),
            P(None, "chan", None, None),
            P(None, "chan", None, None),
        ),
        check_vma=False,
    )
```

profile of v0, /device:TPU:1, one launch (start us, length us, event | category | flops | bytes accessed | tf_op | source)
XLA Modules:
  0.0 1141.6 jit_solution(13108972950838934719)
XLA Ops:
  16.2 104.5 %all-gather.4.cloned.1.call-done = bf16[128,4,32,64]{3,2,0,1:T(8,128)(2,1)} async-done(((bf16[2,4,32,64]{3,2,0,1:T(8,128)(2,1)}), bf16[128,4,32,64]{3,2,0,1:T(8,128)(2,1)}) %all-gather.4.cloned.1.call-update) | async-done | bytes 2097168 | tf_op jit(solution)/shard_map/all_gather | solution.py:161
  120.7 5.6 copy.407
  134.6 4.2 maximum_maximum_fusion
  140.8 3.3 fusion.16
  146.9 3.2 fusion.10
  150.2 15.4 %fusion.25 = f32[2,64,64,64]{3,2,1,0:T(8,128)} fusion(bf16[2,32,64,1]{3,1,2,0:T(8,128)(2,1)S(1)} %copy-done.12, bf16[2,32,64,64]{3,1,2,0:T(8,128)(2,1)S(1)} %copy.410, bf16[64,64,3,3]{1,0,3,2:T(8,128)(2,1)S(1)} %copy-done, s32[]{:T(128)S(6)} %select_n.26, s32[]{:T(128)S(6)} %add.205, s32[]{:T(128)S(6)} %add.206), kind=kOutput, calls=%fused_computation.75 | convolution fusion | flops 34603008 | bytes 4210700 | tf_op jit(solution)/shard_map/oc,ncxy->noxy/dot_general | solution.py:60
  165.6 3.3 fusion.24
  168.9 10.7 bitcast_add_fusion
  179.6 5.7 copy.420
  189.8 47.9 %all_gather.13 = bf16[2,128,32,32]{3,2,0,1:T(8,128)(2,1)} all-gather(bf16[2,64,32,32]{3,2,0,1:T(8,128)(2,1)S(1)} %copy.432), channel_id=1, replica_groups=mesh['tile'=64,'chan'=2] {'chan'}, dimensions={1}, use_global_device_ids=true | all-gather | bytes 786432 | tf_op jit(solution)/shard_map/all_gather | solution.py:171
  237.7 3.3 copy.433
  247.6 6.4 maximum_bitcast_fusion
  253.9 4.3 pad_maximum_fusion
  258.2 3.9 copy.442
  264.1 5.7 fusion.6
  269.7 32.0 %slice.621 = bf16[2,32,32,32]{3,1,2,0:T(8,128)(2,1)} slice(bf16[2,32,64,64]{3,1,2,0:T(8,128)(2,1)} %get-tuple-element.198), slice={[0:2:1], [0:32:1], [0:64:2], [1:64:2]} | slice | bytes 262144 | tf_op jit(solution)/shard_map/slice | solution.py:75
  301.7 32.0 %slice.619 = bf16[2,32,32,32]{3,1,2,0:T(8,128)(2,1)} slice(bf16[2,32,64,64]{3,1,2,0:T(8,128)(2,1)} %get-tuple-element.198), slice={[0:2:1], [0:32:1], [0:64:2], [0:64:2]} | slice | bytes 262144 | tf_op jit(solution)/shard_map/slice | solution.py:75
  333.8 27.9 %slice.625 = bf16[2,32,32,32]{3,1,2,0:T(8,128)(2,1)S(1)} slice(bf16[2,32,64,64]{3,1,2,0:T(8,128)(2,1)} %get-tuple-element.198), slice={[0:2:1], [0:32:1], [1:64:2], [1:64:2]} | slice | bytes 262144 | tf_op jit(solution)/shard_map/slice | solution.py:75
  361.7 32.0 %slice.623 = bf16[2,32,32,32]{3,1,2,0:T(8,128)(2,1)} slice(bf16[2,32,64,64]{3,1,2,0:T(8,128)(2,1)} %get-tuple-element.198), slice={[0:2:1], [0:32:1], [1:64:2], [0:64:2]} | slice | bytes 262144 | tf_op jit(solution)/shard_map/slice | solution.py:75
  414.9 21.4 %all-gather.6.cloned.1.call-done = bf16[2,64,64,64]{3,2,0,1:T(8,128)(2,1)} async-done(((bf16[2,32,64,64]{3,2,0,1:T(8,128)(2,1)}), bf16[2,64,64,64]{3,2,0,1:T(8,128)(2,1)}) %all-gather.6.cloned.1.call-update) | async-done | bytes 1048592 | tf_op jit(solution)/shard_map/all_gather | solution.py:175
  436.3 3.8 convolution_bitcast_fusion.15
  457.8 4.5 copy.510
  462.3 4.4 reshape.665
  467.2 3.7 copy.446
  474.4 3.4 bitcast_add_fusion.5
  477.8 11.3 scatter-add.45
  489.1 5.5 add_select_fusion
  494.6 11.3 scatter-add.46
  506.0 3.6 slice_add_fusion.7
  509.6 23.8 %scatter-add.49 = f32[2,32,66,66]{2,1,0,3:T(8,128)S(1)} dynamic-update-slice(f32[2,32,66,66]{2,1,0,3:T(8,128)S(1)} %scatter-add.46, f32[2,32,64,64]{2,1,0,3:T(8,128)} %slice_add_fusion.7, s32[]{:T(128)} %constant.397.clone.1, s32[]{:T(128)} %constant.397.clone.1, s32[]{:T(128)} %constant.395.clone.1, s32[]{:T(128)} %constant.397.clone.1) | dynamic-update-slice | bytes 2097156 | tf_op jit(solution)/shard_map/scatter-add | solution.py:133
  533.4 3.6 slice_add_fusion.6
  537.0 23.8 %scatter-add.50 = f32[2,32,66,66]{2,1,0,3:T(8,128)S(1)} dynamic-update-slice(f32[2,32,66,66]{2,1,0,3:T(8,128)S(1)} %scatter-add.49, f32[2,32,64,64]{2,1,0,3:T(8,128)} %slice_add_fusion.6, s32[]{:T(128)} %constant.397.clone.1, s32[]{:T(128)} %constant.397.clone.1, s32[]{:T(128)} %constant.395.clone.1, s32[]{:T(128)} %constant.395.clone.1) | dynamic-update-slice | bytes 2097156 | tf_op jit(solution)/shard_map/scatter-add | solution.py:133
  560.8 3.6 slice_add_fusion.5
  564.4 23.8 %scatter-add.51 = f32[2,32,66,66]{2,1,0,3:T(8,128)S(1)} dynamic-update-slice(f32[2,32,66,66]{2,1,0,3:T(8,128)S(1)} %scatter-add.50, f32[2,32,64,64]{2,1,0,3:T(8,128)} %slice_add_fusion.5, s32[]{:T(128)} %constant.397.clone.1, s32[]{:T(128)} %constant.397.clone.1, s32[]{:T(128)} %constant.395.clone.1, s32[]{:T(128)} %constant.411.clone.1) | dynamic-update-slice | bytes 2097156 | tf_op jit(solution)/shard_map/scatter-add | solution.py:133
  588.2 3.6 slice_add_fusion.4
  591.8 23.8 %scatter-add.54 = f32[2,32,66,66]{2,1,0,3:T(8,128)S(1)} dynamic-update-slice(f32[2,32,66,66]{2,1,0,3:T(8,128)S(1)} %scatter-add.51, f32[2,32,64,64]{2,1,0,3:T(8,128)} %slice_add_fusion.4, s32[]{:T(128)} %constant.397.clone.1, s32[]{:T(128)} %constant.397.clone.1, s32[]{:T(128)} %constant.411.clone.1, s32[]{:T(128)} %constant.397.clone.1) | dynamic-update-slice | bytes 2097156 | tf_op jit(solution)/shard_map/scatter-add | solution.py:133
  615.6 3.6 slice_add_fusion.3
  619.2 23.8 %scatter-add.55 = f32[2,32,66,66]{2,1,0,3:T(8,128)S(1)} dynamic-update-slice(f32[2,32,66,66]{2,1,0,3:T(8,128)S(1)} %scatter-add.54, f32[2,32,64,64]{2,1,0,3:T(8,128)} %slice_add_fusion.3, s32[]{:T(128)} %constant.397.clone.1, s32[]{:T(128)} %constant.397.clone.1, s32[]{:T(128)} %constant.411.clone.1, s32[]{:T(128)} %constant.395.clone.1) | dynamic-update-slice | bytes 2097156 | tf_op jit(solution)/shard_map/scatter-add | solution.py:133
  643.0 3.6 slice_add_fusion.2
  646.6 23.9 %scatter-add.56 = f32[2,32,66,66]{2,1,0,3:T(8,128)S(1)} dynamic-update-slice(f32[2,32,66,66]{2,1,0,3:T(8,128)S(1)} %scatter-add.55, f32[2,32,64,64]{2,1,0,3:T(8,128)} %slice_add_fusion.2, s32[]{:T(128)} %constant.397.clone.1, s32[]{:T(128)} %constant.397.clone.1, s32[]{:T(128)} %constant.411.clone.1, s32[]{:T(128)} %constant.411.clone.1) | dynamic-update-slice | bytes 2097156 | tf_op jit(solution)/shard_map/scatter-add | solution.py:133
  679.3 278.6 %all-reduce.4.cloned.1.call-done = (f32[64,32,3,3]{0,1,3,2:T(8,128)}, f32[128,32,2,2]{0,1,3,2:T(8,128)}) async-done(((f32[64,32,3,3]{0,1,3,2:T(8,128)}, f32[128,32,2,2]{0,1,3,2:T(8,128)}), (f32[64,32,3,3]{0,1,3,2:T(8,128)}, f32[128,32,2,2]{0,1,3,2:T(8,128)})) %all-reduce.4.cloned.1.call-update) | async-done | bytes 139280 | tf_op jit(solution)/shard_map/psum | solution.py:177
  959.4 24.5 %reduce-scatter.7.cloned.1.call-done = f32[64,2048]{1,0:T(8,128)} async-done(((f32[128,2048]{1,0:T(8,128)}), f32[64,2048]{1,0:T(8,128)}) %reduce-scatter.7.cloned.1.call-update) | async-done | bytes 524304
  989.7 101.2 %all-gather.8.cloned.1.call-done = bf16[128,4,32,64]{3,2,0,1:T(8,128)(2,1)} async-done(((bf16[2,4,32,64]{3,2,0,1:T(8,128)(2,1)}), bf16[128,4,32,64]{3,2,0,1:T(8,128)(2,1)}) %all-gather.8.cloned.1.call-update) | async-done | bytes 2097168 | tf_op jit(solution)/shard_map/all_gather | solution.py:180
  1090.9 5.5 copy.458
  1102.6 3.6 slice_add_fusion.1
  1109.2 5.2 scatter-add.59
  1114.4 3.6 slice_add_fusion
  1118.0 12.7 %scatter-add.60 = f32[2,32,64,64]{2,1,0,3:T(8,128)S(1)} dynamic-update-slice(f32[2,32,64,64]{2,1,0,3:T(8,128)S(1)} %scatter-add.59, f32[2,32,1,64]{2,1,0,3:T(8,128)} %slice_add_fusion, s32[]{:T(128)} %constant.397.clone.1, s32[]{:T(128)} %constant.397.clone.1, s32[]{:T(128)} %constant.414.clone.1, s32[]{:T(128)} %constant.397.clone.1) | dynamic-update-slice | bytes 32772 | tf_op jit(solution)/shard_map/scatter-add | solution.py:141
  (185 shorter events, 106.5 us)
Async XLA Ops:
  7.2 6.0 copy-start
  7.2 113.5 %all-gather.4.cloned.1.call-start = ((), (), s32[]{:S(2)}) async-start(), calls=%async_computation.2 | async-start | bytes 4259840 | tf_op jit(solution)/shard_map/all_gather | solution.py:161
  9.4 3.3 copy-start.28
  11.6 252.5 %reduce-scatter.5.cloned.1.call-start = ((), (), s32[]{:S(2)}) async-start(), calls=%async_computation.3 | async-start | bytes 6291456 | tf_op jit(solution)/shard_map/reduce_scatter | solution.py:165
  12.9 116.4 %copy-start.29 = (pred[2,4]{0,1:T(4,128)(4,1)}, pred[2,4]{0,1:T(4,128)(4,1)S(1)}, u32[]{:S(2)}) copy-start(pred[2,4]{0,1:T(4,128)(4,1)S(1)} %copy.406) | copy-start | bytes 28
  13.0 116.3 %copy-start.31 = (pred[2,4]{0,1:T(4,128)(4,1)}, pred[2,4]{0,1:T(4,128)(4,1)S(1)}, u32[]{:S(2)}) copy-start(pred[2,4]{0,1:T(4,128)(4,1)S(1)} %copy.405) | copy-start | bytes 28
  13.1 116.2 %copy-start.33 = (pred[2,4]{0,1:T(4,128)(4,1)}, pred[2,4]{0,1:T(4,128)(4,1)S(1)}, u32[]{:S(2)}) copy-start(pred[2,4]{0,1:T(4,128)(4,1)S(1)} %copy.404) | copy-start | bytes 28
  13.1 113.2 %copy-start.27 = (s32[1024]{0:T(1024)}, s32[1024]{0:T(1024)S(1)}, u32[]{:S(2)}) copy-start(s32[1024]{0:T(1024)S(1)} %pad_clamp_fusion) | copy-start | bytes 12292
  138.8 2.1 copy-start.5
  138.8 30.1 %copy-start.7 = (bf16[2,32,65,66]{3,1,2,0:T(8,128)(2,1)}, bf16[2,32,65,66]{3,1,2,0:T(8,128)(2,1)S(1)}, u32[]{:S(2)}) copy-start(bf16[2,32,65,66]{3,1,2,0:T(8,128)(2,1)S(1)} %get-tuple-element.196) | copy-start | bytes 1647364
  146.9 3.3 copy-start.12
  150.2 15.4 %copy-start.10 = (bf16[2,32,64,1]{3,1,2,0:T(8,128)(2,1)S(1)}, bf16[2,32,64,1]{3,1,2,0:T(8,128)(2,1)}, u32[]{:S(2)}) copy-start(bf16[2,32,64,1]{3,1,2,0:T(8,128)(2,1)} %copy.409) | copy-start | bytes 24580
  165.6 3.3 copy-start.4
  185.3 0.9 copy-start.24
  185.3 251.1 %all-gather.6.cloned.1.call-start = ((), (), s32[]{:S(2)}) async-start(), calls=%async_computation.4 | async-start | bytes 3145728 | tf_op jit(solution)/shard_map/all_gather | solution.py:175
  237.7 3.3 copy-start.26
  258.2 5.2 copy-start.35
  393.6 3.7 copy-start.15
  393.6 4.2 copy-start.18
  397.8 4.0 copy-start.14
  399.3 558.6 %all-reduce.4.cloned.1.call-start = ((), (), s32[]{:S(2)}) async-start(), calls=%async_computation.7 | async-start | bytes 425984 | tf_op jit(solution)/shard_map/psum | solution.py:177
  399.7 3.1 copy-start.16
  402.9 2.0 copy-start.19
  404.9 5.8 copy-start.20
  406.1 5.9 copy-start.23
  411.2 2.4 copy-start.22
  412.3 24.1 %copy-start.6 = (bf16[2,32,65,66]{3,1,2,0:T(8,128)(2,1)S(1)}, bf16[2,32,65,66]{3,1,2,0:T(8,128)(2,1)}, u32[]{:S(2)}) copy-start(bf16[2,32,65,66]{3,1,2,0:T(8,128)(2,1)} %copy-done.5) | copy-start | bytes 1647364
  436.3 3.8 copy-start.21
  442.3 1.9 copy-start.13
  444.3 1.8 copy-start.11
  448.4 2.2 copy-start.8
  454.5 2.9 copy-start.17
  457.4 526.6 %reduce-scatter.7.cloned.1.call-start = ((), (), s32[]{:S(2)}) async-start(), calls=%async_computation.6 | async-start | bytes 1572864
  466.7 624.2 %all-gather.8.cloned.1.call-start = ((), (), s32[]{:S(2)}) async-start(), calls=%async_computation.5 | async-start | bytes 4259840 | tf_op jit(solution)/shard_map/all_gather | solution.py:180
  470.9 1.3 copy-start.1
  472.8 1.6 copy-start.2
  670.8 1.5 copy-start.9
  989.7 109.6 %copy-start.30 = (pred[2,4]{0,1:T(4,128)(4,1)S(1)}, pred[2,4]{0,1:T(4,128)(4,1)}, u32[]{:S(2)}) copy-start(pred[2,4]{0,1:T(4,128)(4,1)} %copy-done.29) | copy-start | bytes 28
  989.7 109.6 %copy-start.32 = (pred[2,4]{0,1:T(4,128)(4,1)S(1)}, pred[2,4]{0,1:T(4,128)(4,1)}, u32[]{:S(2)}) copy-start(pred[2,4]{0,1:T(4,128)(4,1)} %copy-done.31) | copy-start | bytes 28
  989.7 109.8 %copy-start.34 = (pred[2,4]{0,1:T(4,128)(4,1)S(1)}, pred[2,4]{0,1:T(4,128)(4,1)}, u32[]{:S(2)}) copy-start(pred[2,4]{0,1:T(4,128)(4,1)} %copy-done.33) | copy-start | bytes 28
  1106.3 2.9 copy-start.3
  1131.0 2.9 copy-start.25
Sparse Core Ops, SparseCore 0:
  11.7 109.0 all-gather.3
  185.4 78.0 reduce-scatter.4
  399.4 36.9 all-gather.5
  457.5 500.3 all-reduce.3
  960.1 23.8 reduce-scatter.6
  985.5 105.3 all-gather.7
where the time goes:
time: 1160 us; the launch traced here: 1140 us
  waiting for transfers between devices  530 us (46%)
  local copies, waits for them, and re-layouts  411 us (35%)
  matrix products  104 us (9%)
  blocking collectives  47.9 us (4%)
  other arithmetic  32.2 us (3%)
  between operations  15 us (1%)
    psum x1, waiting for transfers between devices, on_device(): grad_conv, grad_level = lax.psum((grad_conv, grad_level), 'tile')  279 us
    scatter-add x9, local copies, waits for them, and re-layouts, conv_grads(): grad_padded = grad_padded.at[:, :, row_tap:row_tap + extent, col_tap:col_...  166 us
    slice x8, local copies, waits for them, and re-layouts, conv_two(): hidden[:, :, row_tap::2, col_tap::2].reshape(tile_count, chan_count, -1)  129 us
    all_gather x1, waiting for transfers between devices, on_device(): lax.all_gather(strips, 'tile', axis=0, tiled=True)  105 us
    all_gather x1, waiting for transfers between devices, on_device(): lax.all_gather(rims, 'tile', axis=0, tiled=True)  101 us
    all_gather x1, blocking collectives, on_device(): cot_full = lax.all_gather(cotangent, 'chan', axis=1, tiled=True)  47.9 us
    dot_general x9, matrix products, conv_three(): jnp.einsum('oc,ncxy->noxy', weight[:, :, row_tap, col_tap], padded[:, :,...  43.8 us
    dot_general x9, matrix products, conv_grads(): jnp.einsum('oc,noxy->ncxy', weight[:, :, row_tap, col_tap], grad_full, pr...  31.3 us
  transfers between devices with their start and end apart: 6, of which 5 were waited for; matrix products, arithmetic and copies ran while one was open for 24% of the time, Pallas kernels for 0%

commit v1 on v0

--- a/solution.py
+++ b/solution.py
@@ -4,6 +4,11 @@
 from jax.sharding import PartitionSpec as P
 
 S = 64
+
+
+def gather_over(array, mesh_axis, dim):
+    sent = jnp.stack([array] * lax.axis_size(mesh_axis))
+    return jnp.concatenate(lax.all_to_all(sent, mesh_axis, 0, 0), axis=dim)
 
 
 def edge_strips(source):
@@ -157,9 +162,7 @@
     conv_in = lax.dynamic_slice_in_dim(conv_weight, chan_first, chan_width, 1)
     level_in = lax.dynamic_slice_in_dim(level_weight, chan_first, chan_width, 1)
     strips = edge_strips(inputs)
-    halo_cells = picker(
-        jnp.zeros_like(strips), lax.all_gather(strips, "tile", axis=0, tiled=True), jnp.int32(0)
-    )
+    halo_cells = picker(jnp.zeros_like(strips), gather_over(strips, "tile", 0), jnp.int32(0))
     padded_own = assemble(inputs, orient(halo_cells, gluing))
     partial_pre = conv_three(padded_own, conv_in)
     pre_act = lax.psum_scatter(partial_pre, "chan", scatter_dimension=1, tiled=True)

time: 1160 us -> 1100 us (0.948)
  waiting for transfers between devices: 530 us -> 447 us
    all_gather x1 -> x0, waiting for transfers between devices: 105 us -> none  [on_device(): lax.all_gather(strips, 'tile', axis=0, tiled=True)]
    all_to_all x0 -> x1, waiting for transfers between devices: none -> 24.6 us  [gather_over(): return jnp.concatenate(lax.all_to_all(sent, mesh_axis, 0, 0), axis=dim)]
    unnamed x83 -> x95, local copies, waits for them, and re-layouts: 25.2 us -> 41.3 us
    unnamed x7 -> x6, waiting for transfers between devices: 24.6 us -> 24.6 us
  transfers between devices with their start and end apart: 6 -> 6, of which waited for: 5 -> 5; matrix products, arithmetic and copies ran while one was open for 24% -> 25% of each run, Pallas kernels for 0% -> 0%
where the time goes in v1:
time: 1100 us; the launch traced here: 1080 us
  waiting for transfers between devices  447 us (41%)
  local copies, waits for them, and re-layouts  422 us (38%)
  matrix products  94.2 us (9%)
  blocking collectives  58.6 us (5%)
  other arithmetic  33.8 us (3%)
  between operations  14.7 us (1%)
  starting transfers between devices  12 us (1%)
    psum x1, waiting for transfers between devices, on_device(): grad_conv, grad_level = lax.psum((grad_conv, grad_level), 'tile')  279 us
    scatter-add x9, local copies, waits for them, and re-layouts, conv_grads(): grad_padded = grad_padded.at[:, :, row_tap:row_tap + extent, col_tap:col_...  165 us
    slice x8, local copies, waits for them, and re-layouts, conv_two(): hidden[:, :, row_tap::2, col_tap::2].reshape(tile_count, chan_count, -1)  129 us
    all_gather x1, waiting for transfers between devices, on_device(): lax.all_gather(rims, 'tile', axis=0, tiled=True)  101 us
    all_gather x1, blocking collectives, on_device(): cot_full = lax.all_gather(cotangent, 'chan', axis=1, tiled=True)  58.6 us
    unnamed x95, local copies, waits for them, and re-layouts  41.3 us
    dot_general x9, matrix products, conv_three(): jnp.einsum('oc,ncxy->noxy', weight[:, :, row_tap, col_tap], padded[:, :,...  33.3 us
    dot_general x9, matrix products, conv_grads(): jnp.einsum('oc,noxy->ncxy', weight[:, :, row_tap, col_tap], grad_full, pr...  31.1 us
  transfers between devices with their start and end apart: 6, of which 5 were waited for; matrix products, arithmetic and copies ran while one was open for 25% of the time, Pallas kernels for 0%

profile of v1, /device:TPU:1, one launch (start us, length us, event | category | flops | bytes accessed | tf_op | source)
XLA Modules:
  0.0 1082.4 jit_solution(14326801976286795537)
XLA Ops:
  13.9 7.9 reshape.667
  21.8 11.0 %all-to-all-start = ((bf16[64,2,8192]{2,1,0:T(2,128)(2,1)}), bf16[64,2,8192]{2,1,0:T(2,128)(2,1)}, u32[]{:S(2)}, u32[]{:S(2)}) async-start(bf16[64,2,8192]{2,1,0:T(2,128)(2,1)} %reshape.667), calls=%async_computation | async-start | bytes 4194304 | tf_op jit(solution)/shard_map/all_to_all | solution.py:11
  37.1 24.6 %all-to-all-done = bf16[64,2,8192]{2,1,0:T(2,128)(2,1)} async-done(((bf16[64,2,8192]{2,1,0:T(2,128)(2,1)}), bf16[64,2,8192]{2,1,0:T(2,128)(2,1)}, u32[]{:S(2)}, u32[]{:S(2)}) %all-to-all-start) | async-done | bytes 2097184 | tf_op jit(solution)/shard_map/all_to_all | solution.py:11
  61.7 8.4 reshape.668
  78.4 4.2 maximum_maximum_fusion
  84.6 3.3 fusion.16
  94.0 3.4 fusion.25
  97.4 3.3 fusion.24
  100.7 12.2 %bitcast_add_fusion = f32[2,64,64,64]{1,3,2,0:T(8,128)} fusion(f32[2,64,64,64]{3,2,1,0:T(8,128)} %fusion.10, f32[2,64,64,64]{3,2,1,0:T(8,128)} %fusion.13, f32[2,64,64,64]{3,2,1,0:T(8,128)} %fusion.25, f32[64,2,64,64]{0,3,2,1:T(8,128)S(1)} %copy-done.4, f32[2,64,64,64]{3,2,1,0:T(8,128)} %fusion.24, f32[2,64,64,64]{3,2,1,0:T(8,128)} %fusion.16, ...), kind=kOutput, calls=%fused_computation.3 | convolution fusion | flops 37748736 | bytes 36716552 | tf_op jit(solution)/shard_map/oc,ncxy->noxy/dot_general | solution.py:65
  112.9 5.7 copy.571
  122.2 58.6 %all_gather.9 = bf16[2,128,32,32]{3,2,0,1:T(8,128)(2,1)} all-gather(bf16[2,64,32,32]{3,2,0,1:T(8,128)(2,1)} %copy.583), channel_id=1, replica_groups=mesh['tile'=64,'chan'=2] {'chan'}, dimensions={1}, use_global_device_ids=true | all-gather | bytes 786432 | tf_op jit(solution)/shard_map/all_gather | solution.py:174
  191.3 6.4 maximum_bitcast_fusion
  197.7 4.2 pad_maximum_fusion
  202.0 3.9 copy.593
  207.8 5.7 fusion.6
  213.5 32.0 %slice.621 = bf16[2,32,32,32]{3,1,2,0:T(8,128)(2,1)} slice(bf16[2,32,64,64]{3,1,2,0:T(8,128)(2,1)} %get-tuple-element.206), slice={[0:2:1], [0:32:1], [0:64:2], [1:64:2]} | slice | bytes 262144 | tf_op jit(solution)/shard_map/slice | solution.py:80
  245.5 32.0 %slice.619 = bf16[2,32,32,32]{3,1,2,0:T(8,128)(2,1)} slice(bf16[2,32,64,64]{3,1,2,0:T(8,128)(2,1)} %get-tuple-element.206), slice={[0:2:1], [0:32:1], [0:64:2], [0:64:2]} | slice | bytes 262144 | tf_op jit(solution)/shard_map/slice | solution.py:80
  277.5 27.9 %slice.625 = bf16[2,32,32,32]{3,1,2,0:T(8,128)(2,1)S(1)} slice(bf16[2,32,64,64]{3,1,2,0:T(8,128)(2,1)} %get-tuple-element.206), slice={[0:2:1], [0:32:1], [1:64:2], [1:64:2]} | slice | bytes 262144 | tf_op jit(solution)/shard_map/slice | solution.py:80
  305.4 31.9 %slice.623 = bf16[2,32,32,32]{3,1,2,0:T(8,128)(2,1)} slice(bf16[2,32,64,64]{3,1,2,0:T(8,128)(2,1)} %get-tuple-element.206), slice={[0:2:1], [0:32:1], [1:64:2], [0:64:2]} | slice | bytes 262144 | tf_op jit(solution)/shard_map/slice | solution.py:80
  359.7 17.8 %all-gather.3.cloned.1.call-done = bf16[2,64,64,64]{3,2,0,1:T(8,128)(2,1)} async-done(((bf16[2,32,64,64]{3,2,0,1:T(8,128)(2,1)}), bf16[2,64,64,64]{3,2,0,1:T(8,128)(2,1)}) %all-gather.3.cloned.1.call-update) | async-done | bytes 1048592 | tf_op jit(solution)/shard_map/all_gather | solution.py:178
  377.5 4.1 convolution_bitcast_fusion.15
  399.2 4.5 copy.661
  403.6 4.4 reshape.663
  408.6 3.7 copy.597
  415.8 3.3 bitcast_add_fusion.5
  419.1 11.2 %scatter-add.45 = f32[2,32,66,66]{2,1,0,3:T(8,128)S(1)} dynamic-update-slice(f32[2,32,66,66]{2,1,0,3:T(8,128)S(1)} %scatter-add.44, f32[2,32,64,64]{2,1,0,3:T(8,128)} %bitcast_add_fusion.5, s32[]{:T(128)} %constant.397.clone.1, s32[]{:T(128)} %constant.397.clone.1, s32[]{:T(128)} %bitcast.75, s32[]{:T(128)} %bitcast.76) | dynamic-update-slice | bytes 2097156 | tf_op jit(solution)/shard_map/scatter-add | solution.py:138
  430.2 5.4 add_select_fusion
  435.7 11.2 %scatter-add.46 = f32[2,32,66,66]{2,1,0,3:T(8,128)S(1)} dynamic-update-slice(f32[2,32,66,66]{2,1,0,3:T(8,128)S(1)} %scatter-add.45, f32[2,32,64,64]{2,1,0,3:T(8,128)} %add_select_fusion, s32[]{:T(128)} %constant.397.clone.1, s32[]{:T(128)} %constant.397.clone.1, s32[]{:T(128)} %bitcast.79, s32[]{:T(128)} %bitcast.80) | dynamic-update-slice | bytes 2097156 | tf_op jit(solution)/shard_map/scatter-add | solution.py:138
  446.9 3.6 slice_add_fusion.7
  450.5 23.8 %scatter-add.49 = f32[2,32,66,66]{2,1,0,3:T(8,128)S(1)} dynamic-update-slice(f32[2,32,66,66]{2,1,0,3:T(8,128)S(1)} %scatter-add.46, f32[2,32,64,64]{2,1,0,3:T(8,128)} %slice_add_fusion.7, s32[]{:T(128)} %constant.397.clone.1, s32[]{:T(128)} %constant.397.clone.1, s32[]{:T(128)} %constant.395.clone.1, s32[]{:T(128)} %constant.397.clone.1) | dynamic-update-slice | bytes 2097156 | tf_op jit(solution)/shard_map/scatter-add | solution.py:138
  474.3 3.6 slice_add_fusion.6
  477.9 23.8 %scatter-add.50 = f32[2,32,66,66]{2,1,0,3:T(8,128)S(1)} dynamic-update-slice(f32[2,32,66,66]{2,1,0,3:T(8,128)S(1)} %scatter-add.49, f32[2,32,64,64]{2,1,0,3:T(8,128)} %slice_add_fusion.6, s32[]{:T(128)} %constant.397.clone.1, s32[]{:T(128)} %constant.397.clone.1, s32[]{:T(128)} %constant.395.clone.1, s32[]{:T(128)} %constant.395.clone.1) | dynamic-update-slice | bytes 2097156 | tf_op jit(solution)/shard_map/scatter-add | solution.py:138
  501.7 3.6 slice_add_fusion.5
  505.3 23.8 %scatter-add.51 = f32[2,32,66,66]{2,1,0,3:T(8,128)S(1)} dynamic-update-slice(f32[2,32,66,66]{2,1,0,3:T(8,128)S(1)} %scatter-add.50, f32[2,32,64,64]{2,1,0,3:T(8,128)} %slice_add_fusion.5, s32[]{:T(128)} %constant.397.clone.1, s32[]{:T(128)} %constant.397.clone.1, s32[]{:T(128)} %constant.395.clone.1, s32[]{:T(128)} %constant.411.clone.1) | dynamic-update-slice | bytes 2097156 | tf_op jit(solution)/shard_map/scatter-add | solution.py:138
  529.1 3.6 slice_add_fusion.4
  532.7 23.8 %scatter-add.54 = f32[2,32,66,66]{2,1,0,3:T(8,128)S(1)} dynamic-update-slice(f32[2,32,66,66]{2,1,0,3:T(8,128)S(1)} %scatter-add.51, f32[2,32,64,64]{2,1,0,3:T(8,128)} %slice_add_fusion.4, s32[]{:T(128)} %constant.397.clone.1, s32[]{:T(128)} %constant.397.clone.1, s32[]{:T(128)} %constant.411.clone.1, s32[]{:T(128)} %constant.397.clone.1) | dynamic-update-slice | bytes 2097156 | tf_op jit(solution)/shard_map/scatter-add | solution.py:138
  556.5 3.6 slice_add_fusion.3
  560.1 23.8 %scatter-add.55 = f32[2,32,66,66]{2,1,0,3:T(8,128)S(1)} dynamic-update-slice(f32[2,32,66,66]{2,1,0,3:T(8,128)S(1)} %scatter-add.54, f32[2,32,64,64]{2,1,0,3:T(8,128)} %slice_add_fusion.3, s32[]{:T(128)} %constant.397.clone.1, s32[]{:T(128)} %constant.397.clone.1, s32[]{:T(128)} %constant.411.clone.1, s32[]{:T(128)} %constant.395.clone.1) | dynamic-update-slice | bytes 2097156 | tf_op jit(solution)/shard_map/scatter-add | solution.py:138
  583.9 3.6 slice_add_fusion.2
  587.5 23.9 %scatter-add.56 = f32[2,32,66,66]{2,1,0,3:T(8,128)S(1)} dynamic-update-slice(f32[2,32,66,66]{2,1,0,3:T(8,128)S(1)} %scatter-add.55, f32[2,32,64,64]{2,1,0,3:T(8,128)} %slice_add_fusion.2, s32[]{:T(128)} %constant.397.clone.1, s32[]{:T(128)} %constant.397.clone.1, s32[]{:T(128)} %constant.411.clone.1, s32[]{:T(128)} %constant.411.clone.1) | dynamic-update-slice | bytes 2097156 | tf_op jit(solution)/shard_map/scatter-add | solution.py:138
  620.3 278.8 %all-reduce.4.cloned.1.call-done = (f32[64,32,3,3]{0,1,3,2:T(8,128)}, f32[128,32,2,2]{0,1,3,2:T(8,128)}) async-done(((f32[64,32,3,3]{0,1,3,2:T(8,128)}, f32[128,32,2,2]{0,1,3,2:T(8,128)}), (f32[64,32,3,3]{0,1,3,2:T(8,128)}, f32[128,32,2,2]{0,1,3,2:T(8,128)})) %all-reduce.4.cloned.1.call-update) | async-done | bytes 139280 | tf_op jit(solution)/shard_map/psum | solution.py:180
  900.6 24.5 %reduce-scatter.7.cloned.1.call-done = f32[64,2048]{1,0:T(8,128)} async-done(((f32[128,2048]{1,0:T(8,128)}), f32[64,2048]{1,0:T(8,128)}) %reduce-scatter.7.cloned.1.call-update) | async-done | bytes 524304
  930.9 101.2 %all-gather.5.cloned.1.call-done = bf16[128,4,32,64]{3,2,0,1:T(8,128)(2,1)} async-done(((bf16[2,4,32,64]{3,2,0,1:T(8,128)(2,1)}), bf16[128,4,32,64]{3,2,0,1:T(8,128)(2,1)}) %all-gather.5.cloned.1.call-update) | async-done | bytes 2097168 | tf_op jit(solution)/shard_map/all_gather | solution.py:183
  1032.1 5.5 copy.609
  1043.7 3.6 slice_add_fusion.1
  1050.3 5.2 scatter-add.59
  1055.5 3.6 slice_add_fusion
  1059.2 12.7 %scatter-add.60 = f32[2,32,64,64]{2,1,0,3:T(8,128)S(1)} dynamic-update-slice(f32[2,32,64,64]{2,1,0,3:T(8,128)S(1)} %scatter-add.59, f32[2,32,1,64]{2,1,0,3:T(8,128)} %slice_add_fusion, s32[]{:T(128)} %constant.397.clone.1, s32[]{:T(128)} %constant.397.clone.1, s32[]{:T(128)} %constant.414.clone.1, s32[]{:T(128)} %constant.397.clone.1) | dynamic-update-slice | bytes 32772 | tf_op jit(solution)/shard_map/scatter-add | solution.py:146
  (197 shorter events, 115.7 us)
Async XLA Ops:
  7.2 26.8 %copy-start = (bf16[64,64,3,3]{1,0,3,2:T(8,128)(2,1)S(1)}, bf16[64,64,3,3]{1,0,3,2:T(8,128)(2,1)}, u32[]{:S(2)}) copy-start(bf16[64,64,3,3]{1,0,3,2:T(8,128)(2,1)} %param.35) | copy-start | bytes 221188
  21.8 39.9 %all-to-all-start = ((bf16[64,2,8192]{2,1,0:T(2,128)(2,1)}), bf16[64,2,8192]{2,1,0:T(2,128)(2,1)}, u32[]{:S(2)}, u32[]{:S(2)}) async-start(bf16[64,2,8192]{2,1,0:T(2,128)(2,1)} %reshape.667), calls=%async_computation | async-start | bytes 4194304 | tf_op jit(solution)/shard_map/all_to_all | solution.py:11
  32.8 0.8 copy-start.33
  32.8 175.0 %reduce-scatter.5.cloned.1.call-start = ((), (), s32[]{:S(2)}) async-start(), calls=%async_computation.3 | async-start | bytes 6291456 | tf_op jit(solution)/shard_map/reduce_scatter | solution.py:168
  33.8 39.3 %copy-start.34 = (pred[2,4]{0,1:T(4,128)(4,1)}, pred[2,4]{0,1:T(4,128)(4,1)S(1)}, u32[]{:S(2)}) copy-start(pred[2,4]{0,1:T(4,128)(4,1)S(1)} %copy.557) | copy-start | bytes 28
  33.9 39.2 %copy-start.36 = (pred[2,4]{0,1:T(4,128)(4,1)}, pred[2,4]{0,1:T(4,128)(4,1)S(1)}, u32[]{:S(2)}) copy-start(pred[2,4]{0,1:T(4,128)(4,1)S(1)} %copy.556) | copy-start | bytes 28
  34.0 39.1 %copy-start.38 = (pred[2,4]{0,1:T(4,128)(4,1)}, pred[2,4]{0,1:T(4,128)(4,1)S(1)}, u32[]{:S(2)}) copy-start(pred[2,4]{0,1:T(4,128)(4,1)S(1)} %copy.555) | copy-start | bytes 28
  34.0 36.1 %copy-start.32 = (s32[1024]{0:T(1024)}, s32[1024]{0:T(1024)S(1)}, u32[]{:S(2)}) copy-start(s32[1024]{0:T(1024)S(1)} %pad_clamp_fusion) | copy-start | bytes 12292
  82.6 2.1 copy-start.5
  82.6 8.2 copy-start.7
  90.7 3.2 copy-start.12
  94.0 3.4 copy-start.10
  97.4 3.3 copy-start.4
  118.5 0.9 copy-start.22
  118.6 258.9 %all-gather.3.cloned.1.call-start = ((), (), s32[]{:S(2)}) async-start(), calls=%async_computation.4 | async-start | bytes 3145728 | tf_op jit(solution)/shard_map/all_gather | solution.py:178
  180.8 3.3 copy-start.31
  184.2 0.6 copy-start.30
  184.2 3.9 copy-start.26
  184.2 3.9 copy-start.24
  184.2 5.5 copy-start.28
  202.0 5.1 copy-start.40
  337.4 4.3 copy-start.15
  337.4 5.4 copy-start.18
  342.8 4.6 copy-start.14
  344.2 554.8 %all-reduce.4.cloned.1.call-start = ((), (), s32[]{:S(2)}) async-start(), calls=%async_computation.7 | async-start | bytes 425984 | tf_op jit(solution)/shard_map/psum | solution.py:180
  344.7 3.7 copy-start.16
  348.4 2.0 copy-start.19
  350.4 3.9 copy-start.20
  350.9 7.1 copy-start.29
  354.3 4.1 copy-start.27
  377.5 4.1 copy-start.6
  377.5 4.1 copy-start.21
  383.7 1.9 copy-start.13
  385.6 1.8 copy-start.11
  389.8 2.2 copy-start.8
  395.9 2.9 copy-start.17
  395.9 2.9 copy-start.25
  398.7 526.4 %reduce-scatter.7.cloned.1.call-start = ((), (), s32[]{:S(2)}) async-start(), calls=%async_computation.6 | async-start | bytes 1572864
  408.1 624.0 %all-gather.5.cloned.1.call-start = ((), (), s32[]{:S(2)}) async-start(), calls=%async_computation.5 | async-start | bytes 4259840 | tf_op jit(solution)/shard_map/all_gather | solution.py:183
  412.3 1.3 copy-start.1
  414.2 1.6 copy-start.2
  611.7 1.5 copy-start.9
  930.9 109.6 %copy-start.35 = (pred[2,4]{0,1:T(4,128)(4,1)S(1)}, pred[2,4]{0,1:T(4,128)(4,1)}, u32[]{:S(2)}) copy-start(pred[2,4]{0,1:T(4,128)(4,1)} %copy-done.34) | copy-start | bytes 28
  930.9 109.6 %copy-start.37 = (pred[2,4]{0,1:T(4,128)(4,1)S(1)}, pred[2,4]{0,1:T(4,128)(4,1)}, u32[]{:S(2)}) copy-start(pred[2,4]{0,1:T(4,128)(4,1)} %copy-done.36) | copy-start | bytes 28
  930.9 109.8 %copy-start.39 = (pred[2,4]{0,1:T(4,128)(4,1)S(1)}, pred[2,4]{0,1:T(4,128)(4,1)}, u32[]{:S(2)}) copy-start(pred[2,4]{0,1:T(4,128)(4,1)} %copy-done.38) | copy-start | bytes 28
  1047.4 2.9 copy-start.3
  1072.2 2.9 copy-start.23
Sparse Core Ops, SparseCore 0:
  118.7 78.6 reduce-scatter.4
  344.4 33.0 all-gather.2
  398.9 500.1 all-reduce.3
  901.2 23.8 reduce-scatter.6
  926.7 105.3 all-gather.4
